TPU v7x, 128 devices: a whole 4x4x4 slice. The times are simulated.
128 devices in a mesh: gx: 8 (over x, core), gy: 4 (over y), gz: 4 (over z).
Axes of the slice: x: 4, y: 4, z: 4, core: 2. Of those that a mesh axis runs over, the one named last changes fastest.
Arguments:
- start_block: float32 [16, 32, 64, 512], P(None, 'gx', 'gy', 'gz')
- basis: bfloat16 [256, 32, 64, 512], P(None, 'gx', 'gy', 'gz')
- trans_x: float32 [32, 64, 512], P('gx', 'gy', 'gz'), may hold values from 0.05 to 1
- trans_y: float32 [32, 64, 512], P('gx', 'gy', 'gz'), may hold values from 0.05 to 1
- trans_z: float32 [32, 64, 512], P('gx', 'gy', 'gz'), may hold values from 0.05 to 1
- pore_volume: float32 [32, 64, 512], P('gx', 'gy', 'gz'), may hold values from 0.5 to 2
- shift_table: float32 [16], replicated, may hold values from 0.5 to 4
- shift_index: int32 [1], replicated, may hold values from 0 to 15
- fault_send: int32 [128, 128, 32], P(('gx', 'gy', 'gz')), may hold values from 0 to 8191
- fault_recv: int32 [128, 128, 32], P(('gx', 'gy', 'gz')), may hold values from 0 to 8191
- fault_trans: float32 [128, 128, 32], P(('gx', 'gy', 'gz')), may hold values from 0.05 to 0.5
- well_cells: int32 [64], replicated, may hold values from 0 to 1048575
Outputs:
- new_block: float32 [16, 32, 64, 512], P(None, 'gx', 'gy', 'gz')
- first_coeffs: float32 [256, 16], replicated
- coeffs: float32 [256, 16], replicated
- well_resp: float32 [64, 16], replicated
Inputs may be any that keep to these rules, and one draw needn't show every extreme that they name: fault_send[d, p, s] is a local cell number on device d; the value of that cell feeds a connection into device p. fault_recv[d, p, s] is a local cell number on device d. `well_cells`: flat cell index, last dimension fastest.
All inputs are finite; a program needn't handle non-finite values.
Results may differ from a plain program's by a relative error of at most 0.0065.
Values sent between devices are 32-bit elements; how exact they have to be, the bound alone decides.
A program may use at most 128 MiB of HBM per device.

v0:
```python
import math
import jax
import jax.numpy as jnp
from jax import lax
from jax.sharding import PartitionSpec as P

TERMS = 8


def from_behind(value, axis, by):
    size = lax.axis_size(axis)
    pairs = [(i, i + by) for i in range(size) if 0 <= i + by < size]
    return lax.ppermute(value, axis, pairs)


def extended(value, sides, width):
    for axis, dim in sides:
        size, length = (lax.axis_size(axis), value.shape[dim])
        up = [(i, (i + 1) % size) for i in range(size - 1)]
        down = [(j, i) for i, j in up]
        last = lax.slice_in_dim(value, length - width, length, axis=dim)
        initial = lax.slice_in_dim(value, 0, width, axis=dim)
        before = lax.ppermute(last, axis, up)
        after = lax.ppermute(initial, axis, down)
        value = jnp.concatenate([before, value, after], axis=dim)
    return value


def local(
    start_block,
    basis,
    trans_x,
    trans_y,
    trans_z,
    pore_volume,
    shift_table,
    shift_index,
    fault_send,
    fault_recv,
    fault_trans,
    well_cells,
):
    columns, size_x, size_y, size_z = start_block.shape
    cells = size_x * size_y * size_z
    count_x = lax.axis_size("gx")
    count_y = lax.axis_size("gy")
    count_z = lax.axis_size("gz")
    index_x = lax.axis_index("gx")
    index_y = lax.axis_index("gy")
    index_z = lax.axis_index("gz")
    full_x = size_x * count_x
    full_y = size_y * count_y
    full_z = size_z * count_z
    shape3 = (size_x, size_y, size_z)
    pos_x = lax.broadcasted_iota(jnp.int32, shape3, 0) + index_x * size_x
    pos_y = lax.broadcasted_iota(jnp.int32, shape3, 1) + index_y * size_y
    pos_z = lax.broadcasted_iota(jnp.int32, shape3, 2) + index_z * size_z
    upper_x = jnp.where(pos_x < full_x - 1, trans_x, 0.0)
    upper_y = jnp.where(pos_y < full_y - 1, trans_y, 0.0)
    upper_z = jnp.where(pos_z < full_z - 1, trans_z, 0.0)
    edge_x = from_behind(upper_x[-1:, :, :], "gx", 1)
    edge_y = from_behind(upper_y[:, -1:, :], "gy", 1)
    edge_z = from_behind(upper_z[:, :, -1:], "gz", 1)
    lower_x = jnp.concatenate([edge_x, upper_x[:-1, :, :]], axis=0)
    lower_y = jnp.concatenate([edge_y, upper_y[:, :-1, :]], axis=1)
    lower_z = jnp.concatenate([edge_z, upper_z[:, :, :-1]], axis=2)
    shift = jnp.sum(
        jnp.where(
            jnp.arange(shift_table.shape[0], dtype=jnp.int32) == shift_index[0], shift_table, 0.0
        )
    )
    send_flat = fault_send[0].reshape(-1)
    recv_flat = fault_recv[0].reshape(-1)
    weight_flat = fault_trans[0].reshape(-1)
    fault_diag = jnp.zeros((cells,), jnp.float32).at[recv_flat].add(weight_flat).reshape(shape3)
    diagonal = (
        upper_x + lower_x + upper_y + lower_y + upper_z + lower_z + shift * pore_volume + fault_diag
    )
    sigma = 1.0 / 0.9
    weight_now = 1.0 / sigma
    solution = jnp.zeros_like(start_block)
    residual = start_block
    direction = residual / diagonal
    for number in range(TERMS):
        solution = solution + direction
        if number < TERMS - 1:
            grown = extended(direction, (("gx", 1), ("gy", 2), ("gz", 3)), 1)
            operate_flat = direction.reshape(columns, cells)
            incoming = lax.all_to_all(
                operate_flat[:, send_flat],
                ("gx", "gy", "gz"),
                split_axis=1,
                concat_axis=1,
                tiled=True,
            )
            beside = upper_x * grown[:, 2:, 1:-1, 1:-1] + lower_x * grown[:, :-2, 1:-1, 1:-1]
            beside = (
                beside + upper_y * grown[:, 1:-1, 2:, 1:-1] + lower_y * grown[:, 1:-1, :-2, 1:-1]
            )
            beside = (
                beside + upper_z * grown[:, 1:-1, 1:-1, 2:] + lower_z * grown[:, 1:-1, 1:-1, :-2]
            )
            remote = (
                jnp.zeros((columns, cells), jnp.float32)
                .at[:, recv_flat]
                .add(weight_flat * incoming)
            )
            residual = residual - (diagonal * direction - beside - remote.reshape(direction.shape))
            weight_new = 1.0 / (2.0 * sigma - weight_now)
            direction = weight_new * weight_now * direction + 2.0 * weight_new / 0.9 * (
                residual / diagonal
            )
            weight_now = weight_new
    plane = full_y * full_z
    well_x = well_cells // plane
    well_y = well_cells // full_z % full_y
    well_z = well_cells % full_z
    owned = (
        (well_x // size_x == index_x)
        & (well_y // size_y == index_y)
        & (well_z // size_z == index_z)
    )
    local_cell = (well_x % size_x * size_y + well_y % size_y) * size_z + well_z % size_z
    flat_basis = basis.reshape(basis.shape[0], cells)
    flat_x = solution.reshape(columns, cells)
    first_term = jnp.dot(
        flat_basis, flat_x.astype(jnp.bfloat16).T, preferred_element_type=jnp.float32
    )
    first_coeffs = lax.psum(first_term, ("gx", "gy", "gz"))
    first_rest = flat_x - jnp.dot(
        first_coeffs.astype(jnp.bfloat16).T, flat_basis, preferred_element_type=jnp.float32
    )
    second_term = jnp.dot(
        flat_basis, first_rest.astype(jnp.bfloat16).T, preferred_element_type=jnp.float32
    )
    second_coeffs = lax.psum(second_term, ("gx", "gy", "gz"))
    rest = first_rest - jnp.dot(
        second_coeffs.astype(jnp.bfloat16).T, flat_basis, preferred_element_type=jnp.float32
    )
    gram_term = jnp.dot(rest, rest.T, precision=lax.Precision.HIGHEST)
    gram, wells_value = lax.psum(
        (gram_term, jnp.where(owned[None, :], rest[:, local_cell], 0.0)), ("gx", "gy", "gz")
    )
    lower = jnp.linalg.cholesky(gram)
    scale = math.sqrt(full_x * full_y * full_z)
    new_flat = lax.linalg.triangular_solve(lower, rest, left_side=True, lower=True) * scale
    well_resp = (
        lax.linalg.triangular_solve(lower, wells_value, left_side=True, lower=True) * scale
    ).T
    return (
        new_flat.reshape(start_block.shape),
        first_coeffs,
        first_coeffs + second_coeffs,
        well_resp,
    )


def solution(mesh):
    in_specs = (
        P(None, "gx", "gy", "gz"),
        P(None, "gx", "gy", "gz"),
        P("gx", "gy", "gz"),
        P("gx", "gy", "gz"),
        P("gx", "gy", "gz"),
        P("gx", "gy", "gz"),
        P(),
        P(),
        P(("gx", "gy", "gz"), None, None),
        P(("gx", "gy", "gz"), None, None),
        P(("gx", "gy", "gz"), None, None),
        P(),
    )
    out_specs = (P(None, "gx", "gy", "gz"), P(), P(), P())
    return jax.shard_map(local, mesh=mesh, in_specs=in_specs, out_specs=out_specs, check_vma=False)
```

profile of v0, /device:TPU:1, one launch (start us, length us, event | category | flops | bytes accessed | tf_op | source)
XLA Modules:
  0.0 1015.0 jit_solution(15570318955301733830)
XLA Ops:
  1.6 4.5 collective-permute-start
  19.2 21.9 %scatter_custom_fusion = f32[8192]{0:T(1024)S(1)} fusion(s32[4096]{0:T(1024)S(1)} %bitcast.158, f32[4096]{0:T(1024)S(1)} %reshape.239, f32[]{:T(128)} %constant.173.clone.1), kind=kCustom, calls=%fused_computation.323 | custom fusion | flops 4096 | bytes 32772 | tf_op jit(solution)/shard_map/scatter-add | solution.py:75
  59.0 16.4 %gather_fusion = f32[4096,16]{1,0:T(8,128)} fusion(f32[16,8192]{0,1:T(8,128)} %bitcast.125, s32[4096]{0:T(1024)S(1)} %broadcast_clamp_fusion), kind=kCustom, calls=%fused_computation | custom fusion | bytes 540672 | tf_op jit(solution)/shard_map/gather | solution.py:90
  78.8 11.2 %all-to-all-start = ((f32[128,1,512]{2,1,0:T(1,128)}), f32[128,1,512]{2,1,0:T(1,128)S(1)}, u32[]{:S(2)}, u32[]{:S(2)}) async-start(f32[128,1,512]{2,1,0:T(1,128)} %reshape.317), calls=%async_computation | async-start | bytes 524288 | tf_op jit(solution)/shard_map/all_to_all | solution.py:89
  113.2 25.0 %scatter_custom_fusion.1 = f32[16,8192]{0,1:T(8,128)} fusion(s32[4096]{0:T(1024)} %bitcast.159, f32[4096,16]{1,0:T(8,128)} %copy.299, f32[]{:T(128)} %constant.173.clone.1), kind=kCustom, calls=%fused_computation.40 | custom fusion | flops 65536 | bytes 524800 | tf_op jit(solution)/shard_map/scatter-add | solution.py:106
  161.3 16.4 %gather_fusion.1 = f32[4096,16]{1,0:T(8,128)} fusion(f32[16,8192]{0,1:T(8,128)} %bitcast.126, s32[4096]{0:T(1024)S(1)} %broadcast_clamp_fusion), kind=kCustom, calls=%fused_computation.1 | custom fusion | bytes 540672 | tf_op jit(solution)/shard_map/gather | solution.py:90
  181.0 11.4 %all-to-all-start.1 = ((f32[128,1,512]{2,1,0:T(1,128)}), f32[128,1,512]{2,1,0:T(1,128)}, u32[]{:S(2)}, u32[]{:S(2)}) async-start(f32[128,1,512]{2,1,0:T(1,128)} %reshape.319), calls=%async_computation.1 | async-start | bytes 524288 | tf_op jit(solution)/shard_map/all_to_all | solution.py:89
  216.0 24.8 %scatter_custom_fusion.2 = f32[16,8192]{0,1:T(8,128)} fusion(s32[4096]{0:T(1024)} %bitcast.160, f32[4096,16]{1,0:T(8,128)} %copy.314, f32[]{:T(128)} %constant.173.clone.1), kind=kCustom, calls=%fused_computation.38 | custom fusion | flops 65536 | bytes 524800 | tf_op jit(solution)/shard_map/scatter-add | solution.py:106
  264.2 16.4 %gather_fusion.2 = f32[4096,16]{1,0:T(8,128)} fusion(f32[16,8192]{0,1:T(8,128)} %bitcast.127, s32[4096]{0:T(1024)S(1)} %broadcast_clamp_fusion), kind=kCustom, calls=%fused_computation.2 | custom fusion | bytes 540672 | tf_op jit(solution)/shard_map/gather | solution.py:90
  284.0 11.4 %all-to-all-start.2 = ((f32[128,1,512]{2,1,0:T(1,128)}), f32[128,1,512]{2,1,0:T(1,128)}, u32[]{:S(2)}, u32[]{:S(2)}) async-start(f32[128,1,512]{2,1,0:T(1,128)} %reshape.321), calls=%async_computation.2 | async-start | bytes 524288 | tf_op jit(solution)/shard_map/all_to_all | solution.py:89
  319.0 24.8 %scatter_custom_fusion.3 = f32[16,8192]{0,1:T(8,128)} fusion(s32[4096]{0:T(1024)} %bitcast.161, f32[4096,16]{1,0:T(8,128)} %copy.329, f32[]{:T(128)} %constant.173.clone.1), kind=kCustom, calls=%fused_computation.36 | custom fusion | flops 65536 | bytes 524800 | tf_op jit(solution)/shard_map/scatter-add | solution.py:106
  366.5 16.4 %gather_fusion.3 = f32[4096,16]{1,0:T(8,128)} fusion(f32[16,8192]{0,1:T(8,128)} %bitcast.128, s32[4096]{0:T(1024)S(1)} %broadcast_clamp_fusion), kind=kCustom, calls=%fused_computation.3 | custom fusion | bytes 540672 | tf_op jit(solution)/shard_map/gather | solution.py:90
  386.3 11.4 %all-to-all-start.3 = ((f32[128,1,512]{2,1,0:T(1,128)}), f32[128,1,512]{2,1,0:T(1,128)}, u32[]{:S(2)}, u32[]{:S(2)}) async-start(f32[128,1,512]{2,1,0:T(1,128)} %reshape.323), calls=%async_computation.3 | async-start | bytes 524288 | tf_op jit(solution)/shard_map/all_to_all | solution.py:89
  423.3 24.8 %scatter_custom_fusion.4 = f32[16,8192]{0,1:T(8,128)} fusion(s32[4096]{0:T(1024)} %bitcast.162, f32[4096,16]{1,0:T(8,128)} %copy.344, f32[]{:T(128)} %constant.173.clone.1), kind=kCustom, calls=%fused_computation.34 | custom fusion | flops 65536 | bytes 524800 | tf_op jit(solution)/shard_map/scatter-add | solution.py:106
  466.1 4.6 collective-permute-start.30
  473.4 16.4 %gather_fusion.4 = f32[4096,16]{1,0:T(8,128)} fusion(f32[16,8192]{0,1:T(8,128)} %bitcast.129, s32[4096]{0:T(1024)S(1)} %broadcast_clamp_fusion), kind=kCustom, calls=%fused_computation.4 | custom fusion | bytes 540672 | tf_op jit(solution)/shard_map/gather | solution.py:90
  493.1 10.8 %all-to-all-start.4 = ((f32[128,1,512]{2,1,0:T(1,128)}), f32[128,1,512]{2,1,0:T(1,128)}, u32[]{:S(2)}, u32[]{:S(2)}) async-start(f32[128,1,512]{2,1,0:T(1,128)} %reshape.325), calls=%async_computation.4 | async-start | bytes 524288 | tf_op jit(solution)/shard_map/all_to_all | solution.py:89
  511.4 4.1 collective-permute-start.32
  532.9 24.8 %scatter_custom_fusion.5 = f32[16,8192]{0,1:T(8,128)} fusion(s32[4096]{0:T(1024)} %bitcast.163, f32[4096,16]{1,0:T(8,128)} %copy.359, f32[]{:T(128)} %constant.173.clone.1), kind=kCustom, calls=%fused_computation.32 | custom fusion | flops 65536 | bytes 524800 | tf_op jit(solution)/shard_map/scatter-add | solution.py:106
  575.1 4.6 collective-permute-start.36
  582.4 16.4 %gather_fusion.5 = f32[4096,16]{1,0:T(8,128)} fusion(f32[16,8192]{0,1:T(8,128)} %bitcast.130, s32[4096]{0:T(1024)S(1)} %broadcast_clamp_fusion), kind=kCustom, calls=%fused_computation.5 | custom fusion | bytes 540672 | tf_op jit(solution)/shard_map/gather | solution.py:90
  604.3 9.8 all-to-all-start.5
  639.8 24.8 %scatter_custom_fusion.6 = f32[16,8192]{0,1:T(8,128)} fusion(s32[4096]{0:T(1024)} %bitcast.164, f32[4096,16]{1,0:T(8,128)} %copy.374, f32[]{:T(128)} %constant.173.clone.1), kind=kCustom, calls=%fused_computation.30 | custom fusion | flops 65536 | bytes 524800 | tf_op jit(solution)/shard_map/scatter-add | solution.py:106
  683.5 4.6 collective-permute-start.42
  690.8 16.4 %gather_fusion.6 = f32[4096,16]{1,0:T(8,128)} fusion(f32[16,8192]{0,1:T(8,128)} %bitcast.124, s32[4096]{0:T(1024)S(1)} %broadcast_clamp_fusion), kind=kCustom, calls=%fused_computation.6 | custom fusion | bytes 540672 | tf_op jit(solution)/shard_map/gather | solution.py:90
  712.8 11.4 %all-to-all-start.6 = ((f32[128,1,512]{2,1,0:T(1,128)}), f32[128,1,512]{2,1,0:T(1,128)}, u32[]{:S(2)}, u32[]{:S(2)}) async-start(f32[128,1,512]{2,1,0:T(1,128)} %reshape.329), calls=%async_computation.6 | async-start | bytes 524288 | tf_op jit(solution)/shard_map/all_to_all | solution.py:89
  761.0 24.8 %scatter_custom_fusion.7 = f32[16,8192]{0,1:T(8,128)} fusion(s32[4096]{0:T(1024)} %bitcast.165, f32[4096,16]{1,0:T(8,128)} %copy.389, f32[]{:T(128)} %constant.173.clone.1), kind=kCustom, calls=%fused_computation.28 | custom fusion | flops 65536 | bytes 524800 | tf_op jit(solution)/shard_map/scatter-add | solution.py:106
  795.7 67.1 %psum.28 = f32[256,16]{0,1:T(8,128)S(1)} all-reduce(f32[256,16]{0,1:T(8,128)S(1)} %fusion.24), channel_id=1, replica_groups=mesh['gx'=8,'gy'=4,'gz'=4] {'gx','gy','gz'}, use_global_device_ids=true, to_apply=%region_9.10 | all-reduce | flops 4096 | bytes 32768 | tf_op jit(solution)/shard_map/psum | solution.py:129
  862.8 4.9 convolution_subtract_fusion.1
  870.0 62.8 %psum.29 = f32[256,16]{0,1:T(8,128)S(1)} all-reduce(f32[256,16]{0,1:T(8,128)S(1)} %fusion.27), channel_id=1, replica_groups=mesh['gx'=8,'gy'=4,'gz'=4] {'gx','gy','gz'}, use_global_device_ids=true, to_apply=%region_10.11 | all-reduce | flops 4096 | bytes 32768 | tf_op jit(solution)/shard_map/psum | solution.py:136
  932.8 4.5 convolution_subtract_fusion
  944.2 64.1 %all-reduce = (f32[16,16]{0,1:T(8,128)S(1)}, f32[16,64]{0,1:T(8,128)S(1)}) all-reduce(f32[16,16]{0,1:T(8,128)S(1)} %fusion.165, f32[16,64]{0,1:T(8,128)S(1)} %select_bitcast_fusion), channel_id=1, replica_groups=mesh['gx'=8,'gy'=4,'gz'=4] {'gx','gy','gz'}, use_global_device_ids=true, to_apply=%region_11.12 | all-reduce | flops 1280 | bytes 10240 | tf_op jit(solution)/shard_map/psum | solution.py:141
  (378 shorter events, 398.0 us)
Async XLA Ops:
  1.6 39.6 %collective-permute-start = (f32[1,16,128]{2,1,0:T(8,128)S(1)}, f32[1,16,128]{2,1,0:T(8,128)S(1)}, u32[]{:S(2)}, u32[]{:S(2)}) collective-permute-start(f32[1,16,128]{2,1,0:T(8,128)S(1)} %slice.432), channel_id=1, source_target_pairs={{0,16},{16,32},{32,48},{48,64},{64,80},{80,96},{96,112},{1,17},{17... | collective-permute-start | bytes 24584 | tf_op jit(solution)/shard_map/ppermute | solution.py:13
  6.9 34.3 %collective-permute-start.1 = (f32[4,1,128]{2,1,0:T(1,128)S(1)}, f32[4,1,128]{2,1,0:T(1,128)S(1)}, u32[]{:S(2)}, u32[]{:S(2)}) collective-permute-start(f32[4,1,128]{2,1,0:T(1,128)S(1)} %slice.434), channel_id=1, source_target_pairs={{0,4},{4,8},{8,12},{1,5},{5,9},{9,13},{2,6},{6,10},{10,14},{3,7},{... | collective-permute-start | bytes 6152 | tf_op jit(solution)/shard_map/ppermute | solution.py:13
  11.0 30.2 %collective-permute-start.2 = (f32[4,16,1]{2,1,0:T(8,128)S(1)}, f32[4,16,1]{2,1,0:T(8,128)S(1)}, u32[]{:S(2)}, u32[]{:S(2)}) collective-permute-start(f32[4,16,1]{2,1,0:T(8,128)S(1)} %slice.436), channel_id=1, source_target_pairs={{0,1},{1,2},{2,3},{4,5},{5,6},{6,7},{8,9},{9,10},{10,11},{12,13},{... | collective-permute-start | bytes 776 | tf_op jit(solution)/shard_map/ppermute | solution.py:13
  51.0 38.9 %collective-permute-start.5 = (f32[16,6,1,128]{3,0,2,1:T(8,128)S(1)}, f32[16,6,1,128]{3,0,2,1:T(8,128)S(1)}, u32[]{:S(2)}, u32[]{:S(2)}) collective-permute-start(f32[16,6,1,128]{3,0,2,1:T(8,128)S(1)} %copy.398), channel_id=1, source_target_pairs={{4,0},{8,4},{12,8},{5,1},{9,5},{13,9},{6,2},{10,6},{14,10},{7,3},{... | collective-permute-start | bytes 147464 | tf_op jit(solution)/shard_map/ppermute | solution.py:24
  52.3 37.7 %collective-permute-start.6 = (f32[16,6,1,128]{3,0,2,1:T(8,128)S(1)}, f32[16,6,1,128]{3,0,2,1:T(8,128)S(1)}, u32[]{:S(2)}, u32[]{:S(2)}) collective-permute-start(f32[16,6,1,128]{3,0,2,1:T(8,128)S(1)} %copy.399), channel_id=1, source_target_pairs={{0,4},{4,8},{8,12},{1,5},{5,9},{9,13},{2,6},{6,10},{10,14},{3,7},{... | collective-permute-start | bytes 147464 | tf_op jit(solution)/shard_map/ppermute | solution.py:23
  78.8 23.4 %all-to-all-start = ((f32[128,1,512]{2,1,0:T(1,128)}), f32[128,1,512]{2,1,0:T(1,128)S(1)}, u32[]{:S(2)}, u32[]{:S(2)}) async-start(f32[128,1,512]{2,1,0:T(1,128)} %reshape.317), calls=%async_computation | async-start | bytes 524288 | tf_op jit(solution)/shard_map/all_to_all | solution.py:89
  144.7 7.3 collective-permute-start.9
  153.3 39.2 %collective-permute-start.11 = (f32[16,6,1,128]{3,0,2,1:T(8,128)S(1)}, f32[16,6,1,128]{3,0,2,1:T(8,128)S(1)}, u32[]{:S(2)}, u32[]{:S(2)}) collective-permute-start(f32[16,6,1,128]{3,0,2,1:T(8,128)S(1)} %copy.400), channel_id=1, source_target_pairs={{4,0},{8,4},{12,8},{5,1},{9,5},{13,9},{6,2},{10,6},{14,10},{7,3},{... | collective-permute-start | bytes 147464 | tf_op jit(solution)/shard_map/ppermute | solution.py:24
  154.6 37.9 %collective-permute-start.12 = (f32[16,6,1,128]{3,0,2,1:T(8,128)S(1)}, f32[16,6,1,128]{3,0,2,1:T(8,128)S(1)}, u32[]{:S(2)}, u32[]{:S(2)}) collective-permute-start(f32[16,6,1,128]{3,0,2,1:T(8,128)S(1)} %copy.401), channel_id=1, source_target_pairs={{0,4},{4,8},{8,12},{1,5},{5,9},{9,13},{2,6},{6,10},{10,14},{3,7},{... | collective-permute-start | bytes 147464 | tf_op jit(solution)/shard_map/ppermute | solution.py:23
  181.0 23.5 %all-to-all-start.1 = ((f32[128,1,512]{2,1,0:T(1,128)}), f32[128,1,512]{2,1,0:T(1,128)}, u32[]{:S(2)}, u32[]{:S(2)}) async-start(f32[128,1,512]{2,1,0:T(1,128)} %reshape.319), calls=%async_computation.1 | async-start | bytes 524288 | tf_op jit(solution)/shard_map/all_to_all | solution.py:89
  247.3 7.5 collective-permute-start.15
  256.1 39.4 %collective-permute-start.17 = (f32[16,6,1,128]{3,0,2,1:T(8,128)S(1)}, f32[16,6,1,128]{3,0,2,1:T(8,128)S(1)}, u32[]{:S(2)}, u32[]{:S(2)}) collective-permute-start(f32[16,6,1,128]{3,0,2,1:T(8,128)S(1)} %copy.402), channel_id=1, source_target_pairs={{4,0},{8,4},{12,8},{5,1},{9,5},{13,9},{6,2},{10,6},{14,10},{7,3},{... | collective-permute-start | bytes 147464 | tf_op jit(solution)/shard_map/ppermute | solution.py:24
  257.6 37.9 %collective-permute-start.18 = (f32[16,6,1,128]{3,0,2,1:T(8,128)S(1)}, f32[16,6,1,128]{3,0,2,1:T(8,128)S(1)}, u32[]{:S(2)}, u32[]{:S(2)}) collective-permute-start(f32[16,6,1,128]{3,0,2,1:T(8,128)S(1)} %copy.403), channel_id=1, source_target_pairs={{0,4},{4,8},{8,12},{1,5},{5,9},{9,13},{2,6},{6,10},{10,14},{3,7},{... | collective-permute-start | bytes 147464 | tf_op jit(solution)/shard_map/ppermute | solution.py:23
  284.0 25.2 %all-to-all-start.2 = ((f32[128,1,512]{2,1,0:T(1,128)}), f32[128,1,512]{2,1,0:T(1,128)}, u32[]{:S(2)}, u32[]{:S(2)}) async-start(f32[128,1,512]{2,1,0:T(1,128)} %reshape.321), calls=%async_computation.2 | async-start | bytes 524288 | tf_op jit(solution)/shard_map/all_to_all | solution.py:89
  349.8 7.5 collective-permute-start.21
  358.6 39.2 %collective-permute-start.23 = (f32[16,6,1,128]{3,0,2,1:T(8,128)S(1)}, f32[16,6,1,128]{3,0,2,1:T(8,128)S(1)}, u32[]{:S(2)}, u32[]{:S(2)}) collective-permute-start(f32[16,6,1,128]{3,0,2,1:T(8,128)S(1)} %copy.404), channel_id=1, source_target_pairs={{4,0},{8,4},{12,8},{5,1},{9,5},{13,9},{6,2},{10,6},{14,10},{7,3},{... | collective-permute-start | bytes 147464 | tf_op jit(solution)/shard_map/ppermute | solution.py:24
  359.9 37.9 %collective-permute-start.24 = (f32[16,6,1,128]{3,0,2,1:T(8,128)S(1)}, f32[16,6,1,128]{3,0,2,1:T(8,128)S(1)}, u32[]{:S(2)}, u32[]{:S(2)}) collective-permute-start(f32[16,6,1,128]{3,0,2,1:T(8,128)S(1)} %copy.405), channel_id=1, source_target_pairs={{0,4},{4,8},{8,12},{1,5},{5,9},{9,13},{2,6},{6,10},{10,14},{3,7},{... | collective-permute-start | bytes 147464 | tf_op jit(solution)/shard_map/ppermute | solution.py:23
  386.3 27.2 %all-to-all-start.3 = ((f32[128,1,512]{2,1,0:T(1,128)}), f32[128,1,512]{2,1,0:T(1,128)}, u32[]{:S(2)}, u32[]{:S(2)}) async-start(f32[128,1,512]{2,1,0:T(1,128)} %reshape.323), calls=%async_computation.3 | async-start | bytes 524288 | tf_op jit(solution)/shard_map/all_to_all | solution.py:89
  454.9 7.5 collective-permute-start.27
  464.2 39.8 %collective-permute-start.29 = (f32[16,6,1,128]{3,0,2,1:T(8,128)}, f32[16,6,1,128]{3,0,2,1:T(8,128)}, u32[]{:S(2)}, u32[]{:S(2)}) collective-permute-start(f32[16,6,1,128]{3,0,2,1:T(8,128)} %copy.406), channel_id=1, source_target_pairs={{4,0},{8,4},{12,8},{5,1},{9,5},{13,9},{6,2},{10,6},{14,10},{7,3},{... | collective-permute-start | bytes 147464 | tf_op jit(solution)/shard_map/ppermute | solution.py:24
  466.1 38.7 %collective-permute-start.30 = (f32[16,6,1,128]{3,0,2,1:T(8,128)}, f32[16,6,1,128]{3,0,2,1:T(8,128)}, u32[]{:S(2)}, u32[]{:S(2)}) collective-permute-start(f32[16,6,1,128]{3,0,2,1:T(8,128)} %copy.407), channel_id=1, source_target_pairs={{0,4},{4,8},{8,12},{1,5},{5,9},{9,13},{2,6},{6,10},{10,14},{3,7},{... | collective-permute-start | bytes 147464 | tf_op jit(solution)/shard_map/ppermute | solution.py:23
  493.1 30.5 %all-to-all-start.4 = ((f32[128,1,512]{2,1,0:T(1,128)}), f32[128,1,512]{2,1,0:T(1,128)}, u32[]{:S(2)}, u32[]{:S(2)}) async-start(f32[128,1,512]{2,1,0:T(1,128)} %reshape.325), calls=%async_computation.4 | async-start | bytes 524288 | tf_op jit(solution)/shard_map/all_to_all | solution.py:89
  563.9 7.5 collective-permute-start.33
  573.2 40.9 %collective-permute-start.35 = (f32[16,6,1,128]{3,0,2,1:T(8,128)}, f32[16,6,1,128]{3,0,2,1:T(8,128)S(1)}, u32[]{:S(2)}, u32[]{:S(2)}) collective-permute-start(f32[16,6,1,128]{3,0,2,1:T(8,128)} %copy.408), channel_id=1, source_target_pairs={{4,0},{8,4},{12,8},{5,1},{9,5},{13,9},{6,2},{10,6},{14,10},{7,3},{... | collective-permute-start | bytes 147464 | tf_op jit(solution)/shard_map/ppermute | solution.py:24
  575.1 39.1 %collective-permute-start.36 = (f32[16,6,1,128]{3,0,2,1:T(8,128)}, f32[16,6,1,128]{3,0,2,1:T(8,128)}, u32[]{:S(2)}, u32[]{:S(2)}) collective-permute-start(f32[16,6,1,128]{3,0,2,1:T(8,128)} %copy.409), channel_id=1, source_target_pairs={{0,4},{4,8},{8,12},{1,5},{5,9},{9,13},{2,6},{6,10},{10,14},{3,7},{... | collective-permute-start | bytes 147464 | tf_op jit(solution)/shard_map/ppermute | solution.py:23
  604.3 26.6 %all-to-all-start.5 = ((f32[128,1,512]{2,1,0:T(1,128)}), f32[128,1,512]{2,1,0:T(1,128)S(1)}, u32[]{:S(2)}, u32[]{:S(2)}) async-start(f32[128,1,512]{2,1,0:T(1,128)} %reshape.327), calls=%async_computation.5 | async-start | bytes 524288 | tf_op jit(solution)/shard_map/all_to_all | solution.py:89
  619.0 6.8 collective-permute-start.38
  671.6 7.5 collective-permute-start.39
  681.6 42.6 %collective-permute-start.41 = (f32[16,6,1,128]{3,0,2,1:T(8,128)}, f32[16,6,1,128]{3,0,2,1:T(8,128)}, u32[]{:S(2)}, u32[]{:S(2)}) collective-permute-start(f32[16,6,1,128]{3,0,2,1:T(8,128)} %copy.410), channel_id=1, source_target_pairs={{4,0},{8,4},{12,8},{5,1},{9,5},{13,9},{6,2},{10,6},{14,10},{7,3},{... | collective-permute-start | bytes 147464 | tf_op jit(solution)/shard_map/ppermute | solution.py:24
  683.5 41.6 %collective-permute-start.42 = (f32[16,6,1,128]{3,0,2,1:T(8,128)}, f32[16,6,1,128]{3,0,2,1:T(8,128)}, u32[]{:S(2)}, u32[]{:S(2)}) collective-permute-start(f32[16,6,1,128]{3,0,2,1:T(8,128)} %copy.411), channel_id=1, source_target_pairs={{0,4},{4,8},{8,12},{1,5},{5,9},{9,13},{2,6},{6,10},{10,14},{3,7},{... | collective-permute-start | bytes 147464 | tf_op jit(solution)/shard_map/ppermute | solution.py:23
  712.8 33.5 %all-to-all-start.6 = ((f32[128,1,512]{2,1,0:T(1,128)}), f32[128,1,512]{2,1,0:T(1,128)}, u32[]{:S(2)}, u32[]{:S(2)}) async-start(f32[128,1,512]{2,1,0:T(1,128)} %reshape.329), calls=%async_computation.6 | async-start | bytes 524288 | tf_op jit(solution)/shard_map/all_to_all | solution.py:89
  732.0 8.2 collective-permute-start.44
  (61 other events, 815.7 us)
where the time goes:
time: 1030 us; the launch traced here: 1010 us
  local copies, waits for them, and re-layouts  314 us (30%)
  other arithmetic  251 us (24%)
  starting transfers between devices  209 us (20%)
  blocking collectives  194 us (19%)
  waiting for transfers between devices  28 us (3%)
  matrix products  16.4 us (2%)
    scatter-add x7, other arithmetic, local(): remote = jnp.zeros((columns, cells), jnp.float32).at[:, recv_flat].add(we...  174 us
    gather x7, local copies, waits for them, and re-layouts, local(): operate_flat[:, send_flat]  115 us
    all_to_all x7, starting transfers between devices, local(): lax.all_to_all(operate_flat[:, send_flat], ('gx', 'gy', 'gz'), split_axis...  77.5 us
    ppermute x21, starting transfers between devices, extended(): before = lax.ppermute(last, axis, up)  77 us
    psum x1, blocking collectives, local(): first_coeffs = lax.psum(first_term, ('gx', 'gy', 'gz'))  67.1 us
    psum x1, blocking collectives, local(): lax.psum((gram_term, jnp.where(owned[None, :], rest[:, local_cell], 0.0))...  64.1 us
    psum x1, blocking collectives, local(): second_coeffs = lax.psum(second_term, ('gx', 'gy', 'gz'))  62.8 us
    all_to_all x22, local copies, waits for them, and re-layouts, local(): lax.all_to_all(operate_flat[:, send_flat], ('gx', 'gy', 'gz'), split_axis...  47.2 us
  transfers between devices with their start and end apart: 52, of which 21 were waited for; matrix products, arithmetic and copies ran while one was open for 24% of the time, Pallas kernels for 0%

commit v1 on v0

--- a/solution.py
+++ b/solution.py
@@ -126,7 +126,7 @@
     first_term = jnp.dot(
         flat_basis, flat_x.astype(jnp.bfloat16).T, preferred_element_type=jnp.float32
     )
-    first_coeffs = lax.psum(first_term, ("gx", "gy", "gz"))
+    first_coeffs = lax.psum(lax.psum(first_term, "gx"), ("gy", "gz"))
     first_rest = flat_x - jnp.dot(
         first_coeffs.astype(jnp.bfloat16).T, flat_basis, preferred_element_type=jnp.float32
     )

time: 1030 us -> 1060 us (1.029)
  blocking collectives: 194 us -> 226 us
    psum x1 -> x2, blocking collectives: 67.1 us -> 84 us  [local(): first_coeffs = lax.psum(lax.psum(first_term, 'gx'), ('gy', 'gz'))]
    psum x1, blocking collectives: 62.8 us -> 78.9 us  [local(): second_coeffs = lax.psum(second_term, ('gx', 'gy', 'gz'))]
where the time goes in v1:
time: 1060 us; the launch traced here: 1050 us
  local copies, waits for them, and re-layouts  314 us (30%)
  other arithmetic  251 us (24%)
  blocking collectives  226 us (21%)
  starting transfers between devices  209 us (20%)
  waiting for transfers between devices  28 us (3%)
  matrix products  16.4 us (2%)
    scatter-add x7, other arithmetic, local(): remote = jnp.zeros((columns, cells), jnp.float32).at[:, recv_flat].add(we...  174 us
    gather x7, local copies, waits for them, and re-layouts, local(): operate_flat[:, send_flat]  114 us
    psum x2, blocking collectives, local(): first_coeffs = lax.psum(lax.psum(first_term, 'gx'), ('gy', 'gz'))  84 us
    psum x1, blocking collectives, local(): second_coeffs = lax.psum(second_term, ('gx', 'gy', 'gz'))  78.9 us
    all_to_all x7, starting transfers between devices, local(): lax.all_to_all(operate_flat[:, send_flat], ('gx', 'gy', 'gz'), split_axis...  77.5 us
    ppermute x21, starting transfers between devices, extended(): before = lax.ppermute(last, axis, up)  77.1 us
    psum x1, blocking collectives, local(): lax.psum((gram_term, jnp.where(owned[None, :], rest[:, local_cell], 0.0))...  62.8 us
    all_to_all x22, local copies, waits for them, and re-layouts, local(): lax.all_to_all(operate_flat[:, send_flat], ('gx', 'gy', 'gz'), split_axis...  47.3 us
  transfers between devices with their start and end apart: 52, of which 21 were waited for; matrix products, arithmetic and copies ran while one was open for 24% of the time, Pallas kernels for 0%

profile of v1, /device:TPU:1, one launch (start us, length us, event | category | flops | bytes accessed | tf_op | source)
XLA Modules:
  0.0 1046.3 jit_solution(379598529864744819)
XLA Ops:
  1.6 4.5 collective-permute-start
  19.2 21.9 %scatter_custom_fusion = f32[8192]{0:T(1024)S(1)} fusion(s32[4096]{0:T(1024)S(1)} %bitcast.158, f32[4096]{0:T(1024)S(1)} %reshape.239, f32[]{:T(128)} %constant.173.clone.1), kind=kCustom, calls=%fused_computation.323 | custom fusion | flops 4096 | bytes 32772 | tf_op jit(solution)/shard_map/scatter-add | solution.py:75
  59.0 16.3 %gather_fusion = f32[4096,16]{1,0:T(8,128)} fusion(f32[16,8192]{0,1:T(8,128)} %bitcast.125, s32[4096]{0:T(1024)S(1)} %broadcast_clamp_fusion), kind=kCustom, calls=%fused_computation | custom fusion | bytes 540672 | tf_op jit(solution)/shard_map/gather | solution.py:90
  78.7 11.2 %all-to-all-start = ((f32[128,1,512]{2,1,0:T(1,128)}), f32[128,1,512]{2,1,0:T(1,128)S(1)}, u32[]{:S(2)}, u32[]{:S(2)}) async-start(f32[128,1,512]{2,1,0:T(1,128)} %reshape.317), calls=%async_computation | async-start | bytes 524288 | tf_op jit(solution)/shard_map/all_to_all | solution.py:89
  113.1 25.0 %scatter_custom_fusion.1 = f32[16,8192]{0,1:T(8,128)} fusion(s32[4096]{0:T(1024)} %bitcast.159, f32[4096,16]{1,0:T(8,128)} %copy.299, f32[]{:T(128)} %constant.173.clone.1), kind=kCustom, calls=%fused_computation.40 | custom fusion | flops 65536 | bytes 524800 | tf_op jit(solution)/shard_map/scatter-add | solution.py:106
  161.2 16.3 %gather_fusion.1 = f32[4096,16]{1,0:T(8,128)} fusion(f32[16,8192]{0,1:T(8,128)} %bitcast.126, s32[4096]{0:T(1024)S(1)} %broadcast_clamp_fusion), kind=kCustom, calls=%fused_computation.1 | custom fusion | bytes 540672 | tf_op jit(solution)/shard_map/gather | solution.py:90
  180.9 11.4 %all-to-all-start.1 = ((f32[128,1,512]{2,1,0:T(1,128)}), f32[128,1,512]{2,1,0:T(1,128)}, u32[]{:S(2)}, u32[]{:S(2)}) async-start(f32[128,1,512]{2,1,0:T(1,128)} %reshape.319), calls=%async_computation.1 | async-start | bytes 524288 | tf_op jit(solution)/shard_map/all_to_all | solution.py:89
  215.9 24.9 %scatter_custom_fusion.2 = f32[16,8192]{0,1:T(8,128)} fusion(s32[4096]{0:T(1024)} %bitcast.160, f32[4096,16]{1,0:T(8,128)} %copy.314, f32[]{:T(128)} %constant.173.clone.1), kind=kCustom, calls=%fused_computation.38 | custom fusion | flops 65536 | bytes 524800 | tf_op jit(solution)/shard_map/scatter-add | solution.py:106
  264.1 16.3 %gather_fusion.2 = f32[4096,16]{1,0:T(8,128)} fusion(f32[16,8192]{0,1:T(8,128)} %bitcast.127, s32[4096]{0:T(1024)S(1)} %broadcast_clamp_fusion), kind=kCustom, calls=%fused_computation.2 | custom fusion | bytes 540672 | tf_op jit(solution)/shard_map/gather | solution.py:90
  283.8 11.4 %all-to-all-start.2 = ((f32[128,1,512]{2,1,0:T(1,128)}), f32[128,1,512]{2,1,0:T(1,128)}, u32[]{:S(2)}, u32[]{:S(2)}) async-start(f32[128,1,512]{2,1,0:T(1,128)} %reshape.321), calls=%async_computation.2 | async-start | bytes 524288 | tf_op jit(solution)/shard_map/all_to_all | solution.py:89
  318.8 24.9 %scatter_custom_fusion.3 = f32[16,8192]{0,1:T(8,128)} fusion(s32[4096]{0:T(1024)} %bitcast.161, f32[4096,16]{1,0:T(8,128)} %copy.329, f32[]{:T(128)} %constant.173.clone.1), kind=kCustom, calls=%fused_computation.36 | custom fusion | flops 65536 | bytes 524800 | tf_op jit(solution)/shard_map/scatter-add | solution.py:106
  366.3 16.3 %gather_fusion.3 = f32[4096,16]{1,0:T(8,128)} fusion(f32[16,8192]{0,1:T(8,128)} %bitcast.128, s32[4096]{0:T(1024)S(1)} %broadcast_clamp_fusion), kind=kCustom, calls=%fused_computation.3 | custom fusion | bytes 540672 | tf_op jit(solution)/shard_map/gather | solution.py:90
  386.0 11.4 %all-to-all-start.3 = ((f32[128,1,512]{2,1,0:T(1,128)}), f32[128,1,512]{2,1,0:T(1,128)}, u32[]{:S(2)}, u32[]{:S(2)}) async-start(f32[128,1,512]{2,1,0:T(1,128)} %reshape.323), calls=%async_computation.3 | async-start | bytes 524288 | tf_op jit(solution)/shard_map/all_to_all | solution.py:89
  423.0 24.9 %scatter_custom_fusion.4 = f32[16,8192]{0,1:T(8,128)} fusion(s32[4096]{0:T(1024)} %bitcast.162, f32[4096,16]{1,0:T(8,128)} %copy.344, f32[]{:T(128)} %constant.173.clone.1), kind=kCustom, calls=%fused_computation.34 | custom fusion | flops 65536 | bytes 524800 | tf_op jit(solution)/shard_map/scatter-add | solution.py:106
  465.9 4.6 collective-permute-start.30
  473.1 16.3 %gather_fusion.4 = f32[4096,16]{1,0:T(8,128)} fusion(f32[16,8192]{0,1:T(8,128)} %bitcast.129, s32[4096]{0:T(1024)S(1)} %broadcast_clamp_fusion), kind=kCustom, calls=%fused_computation.4 | custom fusion | bytes 540672 | tf_op jit(solution)/shard_map/gather | solution.py:90
  492.8 10.8 %all-to-all-start.4 = ((f32[128,1,512]{2,1,0:T(1,128)}), f32[128,1,512]{2,1,0:T(1,128)}, u32[]{:S(2)}, u32[]{:S(2)}) async-start(f32[128,1,512]{2,1,0:T(1,128)} %reshape.325), calls=%async_computation.4 | async-start | bytes 524288 | tf_op jit(solution)/shard_map/all_to_all | solution.py:89
  532.5 24.9 %scatter_custom_fusion.5 = f32[16,8192]{0,1:T(8,128)} fusion(s32[4096]{0:T(1024)} %bitcast.163, f32[4096,16]{1,0:T(8,128)} %copy.359, f32[]{:T(128)} %constant.173.clone.1), kind=kCustom, calls=%fused_computation.32 | custom fusion | flops 65536 | bytes 524800 | tf_op jit(solution)/shard_map/scatter-add | solution.py:106
  574.8 4.6 collective-permute-start.36
  582.1 16.3 %gather_fusion.5 = f32[4096,16]{1,0:T(8,128)} fusion(f32[16,8192]{0,1:T(8,128)} %bitcast.130, s32[4096]{0:T(1024)S(1)} %broadcast_clamp_fusion), kind=kCustom, calls=%fused_computation.5 | custom fusion | bytes 540672 | tf_op jit(solution)/shard_map/gather | solution.py:90
  604.0 9.8 all-to-all-start.5
  639.4 24.9 %scatter_custom_fusion.6 = f32[16,8192]{0,1:T(8,128)} fusion(s32[4096]{0:T(1024)} %bitcast.164, f32[4096,16]{1,0:T(8,128)} %copy.374, f32[]{:T(128)} %constant.173.clone.1), kind=kCustom, calls=%fused_computation.30 | custom fusion | flops 65536 | bytes 524800 | tf_op jit(solution)/shard_map/scatter-add | solution.py:106
  683.1 4.6 collective-permute-start.42
  690.4 16.3 %gather_fusion.6 = f32[4096,16]{1,0:T(8,128)} fusion(f32[16,8192]{0,1:T(8,128)} %bitcast.124, s32[4096]{0:T(1024)S(1)} %broadcast_clamp_fusion), kind=kCustom, calls=%fused_computation.6 | custom fusion | bytes 540672 | tf_op jit(solution)/shard_map/gather | solution.py:90
  712.3 11.4 %all-to-all-start.6 = ((f32[128,1,512]{2,1,0:T(1,128)}), f32[128,1,512]{2,1,0:T(1,128)}, u32[]{:S(2)}, u32[]{:S(2)}) async-start(f32[128,1,512]{2,1,0:T(1,128)} %reshape.329), calls=%async_computation.6 | async-start | bytes 524288 | tf_op jit(solution)/shard_map/all_to_all | solution.py:89
  760.6 24.9 %scatter_custom_fusion.7 = f32[16,8192]{0,1:T(8,128)} fusion(s32[4096]{0:T(1024)} %bitcast.165, f32[4096,16]{1,0:T(8,128)} %copy.389, f32[]{:T(128)} %constant.173.clone.1), kind=kCustom, calls=%fused_computation.28 | custom fusion | flops 65536 | bytes 524800 | tf_op jit(solution)/shard_map/scatter-add | solution.py:106
  795.3 22.7 %psum.35 = f32[256,16]{0,1:T(8,128)S(1)} all-reduce(f32[256,16]{0,1:T(8,128)S(1)} %fusion.24), channel_id=1, replica_groups=mesh['gx'=8,'gy'=4,'gz'=4] {'gx'}, use_global_device_ids=true, to_apply=%region_9.10 | all-reduce | flops 4096 | bytes 32768 | tf_op jit(solution)/shard_map/psum | solution.py:129
  818.0 61.3 %psum.36 = f32[256,16]{0,1:T(8,128)S(1)} all-reduce(f32[256,16]{0,1:T(8,128)S(1)} %psum.35), channel_id=1, replica_groups=mesh['gx'=8,'gy'=4,'gz'=4] {'gy','gz'}, use_global_device_ids=true, to_apply=%region_10.11 | all-reduce | flops 4096 | bytes 32768 | tf_op jit(solution)/shard_map/psum | solution.py:129
  879.3 4.9 convolution_subtract_fusion.1
  886.5 78.9 %psum.37 = f32[256,16]{0,1:T(8,128)S(1)} all-reduce(f32[256,16]{0,1:T(8,128)S(1)} %fusion.27), channel_id=1, replica_groups=mesh['gx'=8,'gy'=4,'gz'=4] {'gx','gy','gz'}, use_global_device_ids=true, to_apply=%region_11.12 | all-reduce | flops 4096 | bytes 32768 | tf_op jit(solution)/shard_map/psum | solution.py:136
  965.4 4.5 convolution_subtract_fusion
  976.8 62.8 %all-reduce = (f32[16,16]{0,1:T(8,128)S(1)}, f32[16,64]{0,1:T(8,128)S(1)}) all-reduce(f32[16,16]{0,1:T(8,128)S(1)} %fusion.165, f32[16,64]{0,1:T(8,128)S(1)} %select_bitcast_fusion), channel_id=1, replica_groups=mesh['gx'=8,'gy'=4,'gz'=4] {'gx','gy','gz'}, use_global_device_ids=true, to_apply=%region_12.13 | all-reduce | flops 1280 | bytes 10240 | tf_op jit(solution)/shard_map/psum | solution.py:141
  (379 shorter events, 402.4 us)
Async XLA Ops:
  1.6 39.6 %collective-permute-start = (f32[1,16,128]{2,1,0:T(8,128)S(1)}, f32[1,16,128]{2,1,0:T(8,128)S(1)}, u32[]{:S(2)}, u32[]{:S(2)}) collective-permute-start(f32[1,16,128]{2,1,0:T(8,128)S(1)} %slice.432), channel_id=1, source_target_pairs={{0,16},{16,32},{32,48},{48,64},{64,80},{80,96},{96,112},{1,17},{17... | collective-permute-start | bytes 24584 | tf_op jit(solution)/shard_map/ppermute | solution.py:13
  6.9 34.3 %collective-permute-start.1 = (f32[4,1,128]{2,1,0:T(1,128)S(1)}, f32[4,1,128]{2,1,0:T(1,128)S(1)}, u32[]{:S(2)}, u32[]{:S(2)}) collective-permute-start(f32[4,1,128]{2,1,0:T(1,128)S(1)} %slice.434), channel_id=1, source_target_pairs={{0,4},{4,8},{8,12},{1,5},{5,9},{9,13},{2,6},{6,10},{10,14},{3,7},{... | collective-permute-start | bytes 6152 | tf_op jit(solution)/shard_map/ppermute | solution.py:13
  11.0 30.2 %collective-permute-start.2 = (f32[4,16,1]{2,1,0:T(8,128)S(1)}, f32[4,16,1]{2,1,0:T(8,128)S(1)}, u32[]{:S(2)}, u32[]{:S(2)}) collective-permute-start(f32[4,16,1]{2,1,0:T(8,128)S(1)} %slice.436), channel_id=1, source_target_pairs={{0,1},{1,2},{2,3},{4,5},{5,6},{6,7},{8,9},{9,10},{10,11},{12,13},{... | collective-permute-start | bytes 776 | tf_op jit(solution)/shard_map/ppermute | solution.py:13
  51.0 38.8 %collective-permute-start.5 = (f32[16,6,1,128]{3,0,2,1:T(8,128)S(1)}, f32[16,6,1,128]{3,0,2,1:T(8,128)S(1)}, u32[]{:S(2)}, u32[]{:S(2)}) collective-permute-start(f32[16,6,1,128]{3,0,2,1:T(8,128)S(1)} %copy.398), channel_id=1, source_target_pairs={{4,0},{8,4},{12,8},{5,1},{9,5},{13,9},{6,2},{10,6},{14,10},{7,3},{... | collective-permute-start | bytes 147464 | tf_op jit(solution)/shard_map/ppermute | solution.py:24
  52.3 37.6 %collective-permute-start.6 = (f32[16,6,1,128]{3,0,2,1:T(8,128)S(1)}, f32[16,6,1,128]{3,0,2,1:T(8,128)S(1)}, u32[]{:S(2)}, u32[]{:S(2)}) collective-permute-start(f32[16,6,1,128]{3,0,2,1:T(8,128)S(1)} %copy.399), channel_id=1, source_target_pairs={{0,4},{4,8},{8,12},{1,5},{5,9},{9,13},{2,6},{6,10},{10,14},{3,7},{... | collective-permute-start | bytes 147464 | tf_op jit(solution)/shard_map/ppermute | solution.py:23
  78.7 23.4 %all-to-all-start = ((f32[128,1,512]{2,1,0:T(1,128)}), f32[128,1,512]{2,1,0:T(1,128)S(1)}, u32[]{:S(2)}, u32[]{:S(2)}) async-start(f32[128,1,512]{2,1,0:T(1,128)} %reshape.317), calls=%async_computation | async-start | bytes 524288 | tf_op jit(solution)/shard_map/all_to_all | solution.py:89
  144.6 7.3 collective-permute-start.9
  153.2 39.1 %collective-permute-start.11 = (f32[16,6,1,128]{3,0,2,1:T(8,128)S(1)}, f32[16,6,1,128]{3,0,2,1:T(8,128)S(1)}, u32[]{:S(2)}, u32[]{:S(2)}) collective-permute-start(f32[16,6,1,128]{3,0,2,1:T(8,128)S(1)} %copy.400), channel_id=1, source_target_pairs={{4,0},{8,4},{12,8},{5,1},{9,5},{13,9},{6,2},{10,6},{14,10},{7,3},{... | collective-permute-start | bytes 147464 | tf_op jit(solution)/shard_map/ppermute | solution.py:24
  154.5 37.9 %collective-permute-start.12 = (f32[16,6,1,128]{3,0,2,1:T(8,128)S(1)}, f32[16,6,1,128]{3,0,2,1:T(8,128)S(1)}, u32[]{:S(2)}, u32[]{:S(2)}) collective-permute-start(f32[16,6,1,128]{3,0,2,1:T(8,128)S(1)} %copy.401), channel_id=1, source_target_pairs={{0,4},{4,8},{8,12},{1,5},{5,9},{9,13},{2,6},{6,10},{10,14},{3,7},{... | collective-permute-start | bytes 147464 | tf_op jit(solution)/shard_map/ppermute | solution.py:23
  180.9 23.6 %all-to-all-start.1 = ((f32[128,1,512]{2,1,0:T(1,128)}), f32[128,1,512]{2,1,0:T(1,128)}, u32[]{:S(2)}, u32[]{:S(2)}) async-start(f32[128,1,512]{2,1,0:T(1,128)} %reshape.319), calls=%async_computation.1 | async-start | bytes 524288 | tf_op jit(solution)/shard_map/all_to_all | solution.py:89
  247.2 7.5 collective-permute-start.15
  255.9 39.3 %collective-permute-start.17 = (f32[16,6,1,128]{3,0,2,1:T(8,128)S(1)}, f32[16,6,1,128]{3,0,2,1:T(8,128)S(1)}, u32[]{:S(2)}, u32[]{:S(2)}) collective-permute-start(f32[16,6,1,128]{3,0,2,1:T(8,128)S(1)} %copy.402), channel_id=1, source_target_pairs={{4,0},{8,4},{12,8},{5,1},{9,5},{13,9},{6,2},{10,6},{14,10},{7,3},{... | collective-permute-start | bytes 147464 | tf_op jit(solution)/shard_map/ppermute | solution.py:24
  257.5 37.9 %collective-permute-start.18 = (f32[16,6,1,128]{3,0,2,1:T(8,128)S(1)}, f32[16,6,1,128]{3,0,2,1:T(8,128)S(1)}, u32[]{:S(2)}, u32[]{:S(2)}) collective-permute-start(f32[16,6,1,128]{3,0,2,1:T(8,128)S(1)} %copy.403), channel_id=1, source_target_pairs={{0,4},{4,8},{8,12},{1,5},{5,9},{9,13},{2,6},{6,10},{10,14},{3,7},{... | collective-permute-start | bytes 147464 | tf_op jit(solution)/shard_map/ppermute | solution.py:23
  283.8 25.2 %all-to-all-start.2 = ((f32[128,1,512]{2,1,0:T(1,128)}), f32[128,1,512]{2,1,0:T(1,128)}, u32[]{:S(2)}, u32[]{:S(2)}) async-start(f32[128,1,512]{2,1,0:T(1,128)} %reshape.321), calls=%async_computation.2 | async-start | bytes 524288 | tf_op jit(solution)/shard_map/all_to_all | solution.py:89
  349.6 7.5 collective-permute-start.21
  358.4 39.1 %collective-permute-start.23 = (f32[16,6,1,128]{3,0,2,1:T(8,128)S(1)}, f32[16,6,1,128]{3,0,2,1:T(8,128)S(1)}, u32[]{:S(2)}, u32[]{:S(2)}) collective-permute-start(f32[16,6,1,128]{3,0,2,1:T(8,128)S(1)} %copy.404), channel_id=1, source_target_pairs={{4,0},{8,4},{12,8},{5,1},{9,5},{13,9},{6,2},{10,6},{14,10},{7,3},{... | collective-permute-start | bytes 147464 | tf_op jit(solution)/shard_map/ppermute | solution.py:24
  359.7 37.8 %collective-permute-start.24 = (f32[16,6,1,128]{3,0,2,1:T(8,128)S(1)}, f32[16,6,1,128]{3,0,2,1:T(8,128)S(1)}, u32[]{:S(2)}, u32[]{:S(2)}) collective-permute-start(f32[16,6,1,128]{3,0,2,1:T(8,128)S(1)} %copy.405), channel_id=1, source_target_pairs={{0,4},{4,8},{8,12},{1,5},{5,9},{9,13},{2,6},{6,10},{10,14},{3,7},{... | collective-permute-start | bytes 147464 | tf_op jit(solution)/shard_map/ppermute | solution.py:23
  386.0 27.2 %all-to-all-start.3 = ((f32[128,1,512]{2,1,0:T(1,128)}), f32[128,1,512]{2,1,0:T(1,128)}, u32[]{:S(2)}, u32[]{:S(2)}) async-start(f32[128,1,512]{2,1,0:T(1,128)} %reshape.323), calls=%async_computation.3 | async-start | bytes 524288 | tf_op jit(solution)/shard_map/all_to_all | solution.py:89
  454.6 7.5 collective-permute-start.27
  464.0 39.6 %collective-permute-start.29 = (f32[16,6,1,128]{3,0,2,1:T(8,128)}, f32[16,6,1,128]{3,0,2,1:T(8,128)}, u32[]{:S(2)}, u32[]{:S(2)}) collective-permute-start(f32[16,6,1,128]{3,0,2,1:T(8,128)} %copy.406), channel_id=1, source_target_pairs={{4,0},{8,4},{12,8},{5,1},{9,5},{13,9},{6,2},{10,6},{14,10},{7,3},{... | collective-permute-start | bytes 147464 | tf_op jit(solution)/shard_map/ppermute | solution.py:24
  465.9 38.6 %collective-permute-start.30 = (f32[16,6,1,128]{3,0,2,1:T(8,128)}, f32[16,6,1,128]{3,0,2,1:T(8,128)}, u32[]{:S(2)}, u32[]{:S(2)}) collective-permute-start(f32[16,6,1,128]{3,0,2,1:T(8,128)} %copy.407), channel_id=1, source_target_pairs={{0,4},{4,8},{8,12},{1,5},{5,9},{9,13},{2,6},{6,10},{10,14},{3,7},{... | collective-permute-start | bytes 147464 | tf_op jit(solution)/shard_map/ppermute | solution.py:23
  492.8 30.5 %all-to-all-start.4 = ((f32[128,1,512]{2,1,0:T(1,128)}), f32[128,1,512]{2,1,0:T(1,128)}, u32[]{:S(2)}, u32[]{:S(2)}) async-start(f32[128,1,512]{2,1,0:T(1,128)} %reshape.325), calls=%async_computation.4 | async-start | bytes 524288 | tf_op jit(solution)/shard_map/all_to_all | solution.py:89
  563.5 7.5 collective-permute-start.33
  572.9 40.8 %collective-permute-start.35 = (f32[16,6,1,128]{3,0,2,1:T(8,128)}, f32[16,6,1,128]{3,0,2,1:T(8,128)S(1)}, u32[]{:S(2)}, u32[]{:S(2)}) collective-permute-start(f32[16,6,1,128]{3,0,2,1:T(8,128)} %copy.408), channel_id=1, source_target_pairs={{4,0},{8,4},{12,8},{5,1},{9,5},{13,9},{6,2},{10,6},{14,10},{7,3},{... | collective-permute-start | bytes 147464 | tf_op jit(solution)/shard_map/ppermute | solution.py:24
  574.8 39.0 %collective-permute-start.36 = (f32[16,6,1,128]{3,0,2,1:T(8,128)}, f32[16,6,1,128]{3,0,2,1:T(8,128)}, u32[]{:S(2)}, u32[]{:S(2)}) collective-permute-start(f32[16,6,1,128]{3,0,2,1:T(8,128)} %copy.409), channel_id=1, source_target_pairs={{0,4},{4,8},{8,12},{1,5},{5,9},{9,13},{2,6},{6,10},{10,14},{3,7},{... | collective-permute-start | bytes 147464 | tf_op jit(solution)/shard_map/ppermute | solution.py:23
  604.0 26.6 %all-to-all-start.5 = ((f32[128,1,512]{2,1,0:T(1,128)}), f32[128,1,512]{2,1,0:T(1,128)S(1)}, u32[]{:S(2)}, u32[]{:S(2)}) async-start(f32[128,1,512]{2,1,0:T(1,128)} %reshape.327), calls=%async_computation.5 | async-start | bytes 524288 | tf_op jit(solution)/shard_map/all_to_all | solution.py:89
  618.6 6.8 collective-permute-start.38
  671.2 7.5 collective-permute-start.39
  681.2 42.5 %collective-permute-start.41 = (f32[16,6,1,128]{3,0,2,1:T(8,128)}, f32[16,6,1,128]{3,0,2,1:T(8,128)}, u32[]{:S(2)}, u32[]{:S(2)}) collective-permute-start(f32[16,6,1,128]{3,0,2,1:T(8,128)} %copy.410), channel_id=1, source_target_pairs={{4,0},{8,4},{12,8},{5,1},{9,5},{13,9},{6,2},{10,6},{14,10},{7,3},{... | collective-permute-start | bytes 147464 | tf_op jit(solution)/shard_map/ppermute | solution.py:24
  683.1 41.5 %collective-permute-start.42 = (f32[16,6,1,128]{3,0,2,1:T(8,128)}, f32[16,6,1,128]{3,0,2,1:T(8,128)}, u32[]{:S(2)}, u32[]{:S(2)}) collective-permute-start(f32[16,6,1,128]{3,0,2,1:T(8,128)} %copy.411), channel_id=1, source_target_pairs={{0,4},{4,8},{8,12},{1,5},{5,9},{9,13},{2,6},{6,10},{10,14},{3,7},{... | collective-permute-start | bytes 147464 | tf_op jit(solution)/shard_map/ppermute | solution.py:23
  712.3 33.5 %all-to-all-start.6 = ((f32[128,1,512]{2,1,0:T(1,128)}), f32[128,1,512]{2,1,0:T(1,128)}, u32[]{:S(2)}, u32[]{:S(2)}) async-start(f32[128,1,512]{2,1,0:T(1,128)} %reshape.329), calls=%async_computation.6 | async-start | bytes 524288 | tf_op jit(solution)/shard_map/all_to_all | solution.py:89
  731.5 8.2 collective-permute-start.44
  (61 other events, 847.8 us)
